TPU v7x, 256 devices: a whole 4x4x8 slice. The times are simulated.
256 devices in a mesh: seq: 32 (over x, z), head: 8 (over y, core).
Axes of the slice: x: 4, y: 4, z: 8, core: 2. Of those that a mesh axis runs over, the one named last changes fastest.
Arguments:
- queries: bfloat16 [32768, 5120], P('seq', 'head')
- keys: bfloat16 [32768, 5120], P('seq', 'head')
- values: bfloat16 [32768, 5120], P('seq', 'head'), may hold values from -6 to 6
- query_gain: float32 [5120], P('head'), may hold values from 0.1 to 1.9
- key_gain: float32 [5120], P('head'), may hold values from 0.1 to 1.9
- shapes: int32 [8, 3], replicated, may hold values from 4 to 32, as said below
- windows: int32 [256, 27], P('seq'), may hold values from -1 to 255, as said below
- text_keys: bfloat16 [32, 256, 5120], P(None, 'seq', 'head')
- text_values: bfloat16 [32, 256, 5120], P(None, 'seq', 'head'), may hold values from -6 to 6
- owner: int32 [8], replicated, may hold values from 0 to 31, as said below
Outputs:
- attended: bfloat16 [32768, 5120], P('seq', 'head')
Inputs may be any that keep to these rules, and one draw needn't show every extreme that they name: `shapes`: row s is (frames, height, width) of video s in tokens: height and width are 16 and 32, or 32 and 16, so a frame has 4 tiles; each video has from 16 to 48 tiles, and the videos' tiles add up to 256, so no tile holds tokens of two videos. `windows`: entry k of row g stands for the tile k // 9 - 1 frames, (k // 3) % 3 - 1 tile rows and k % 3 - 1 tile columns away from tile g in its video: it holds that tile's number or -1; it is -1 wherever that tile lies outside the video, and entry 13 is always g. `owner`: no two videos share a panel.
All inputs are finite; a program needn't handle non-finite values.
Results may differ from a plain program's by a relative error of at most 0.012.
Values may be sent and summed in bfloat16 or wider, within the bound.
A program may use at most 128 MiB of HBM per device.

v0:
```python
import jax
import jax.numpy as jnp
from jax import lax
from jax.sharding import PartitionSpec as P

HEAD_DIM = 128
D = 5120
TILE_H = 8
TILE_W = 16
REACH = 7
TXT = 256


epsilon = 1e-06


def extended_2(cells, sides, width):
    for axis, dim in sides:
        count = lax.axis_size(axis)
        ends = count - 1
        head = lax.slice_in_dim(cells, 0, width, axis=dim)
        tail = lax.slice_in_dim(cells, cells.shape[dim] - width, cells.shape[dim], axis=dim)
        cells = jnp.concatenate(
            [
                lax.ppermute(tail, axis, [(i, (i + 1) % count) for i in range(ends)]),
                cells,
                lax.ppermute(head, axis, [((i + 1) % count, i) for i in range(ends)]),
            ],
            axis=dim,
        )
    return cells


def tile_table(shape_rows):
    per_frame = shape_rows[:, 1] // TILE_H * (shape_rows[:, 2] // TILE_W)
    tile_counts = shape_rows[:, 0] * per_frame
    tile_ends = jnp.cumsum(tile_counts)
    return (tile_ends - tile_counts, tile_ends)


def locate(tile_ids, shape_rows, tile_starts, tile_ends):
    sample_ids = jnp.sum((tile_ids[:, None] >= tile_ends[None, :]).astype(jnp.int32), axis=1)
    one_hot = (
        sample_ids[:, None] == jnp.arange(tile_ends.shape[0], dtype=jnp.int32)[None, :]
    ).astype(jnp.int32)
    first_tiles = jnp.sum(one_hot * tile_starts[None, :], axis=1)
    row_counts = jnp.sum(one_hot * (shape_rows[:, 1] // TILE_H)[None, :], axis=1)
    col_counts = jnp.sum(one_hot * (shape_rows[:, 2] // TILE_W)[None, :], axis=1)
    offsets = tile_ids - first_tiles
    per_frame = row_counts * col_counts
    within = offsets % per_frame
    return (sample_ids, one_hot, offsets // per_frame, within // col_counts, within % col_counts)


def rope_angles(frames, bands, columns, head_size):
    inner = jnp.arange(TILE_H * TILE_W, dtype=jnp.int32)
    tile_total = frames.shape[0]
    time_pos = (
        jnp.broadcast_to(frames[:, None], (tile_total, inner.shape[0]))
        .reshape(-1)
        .astype(jnp.float32)
    )
    row_pos = (bands[:, None] * TILE_H + inner[None, :] // TILE_W).reshape(-1).astype(jnp.float32)
    col_pos = (columns[:, None] * TILE_W + inner[None, :] % TILE_W).reshape(-1).astype(jnp.float32)
    third = head_size // 6
    part_sizes = (head_size - 4 * third, 2 * third, 2 * third)
    angle_parts = []
    for position, part_size in zip((time_pos, row_pos, col_pos), part_sizes):
        frequency = 10000.0 ** (-jnp.arange(0, part_size, 2, dtype=jnp.float32) / part_size)
        angle_parts.append(position[:, None] * frequency[None, :])
    return jnp.concatenate(angle_parts, axis=1)


def rotate(field, angles):
    paired = field.reshape(field.shape[0], field.shape[1], field.shape[2] // 2, 2)
    cosine = jnp.cos(angles)[:, None, :]
    sine = jnp.sin(angles)[:, None, :]
    even_part = paired[..., 0]
    odd_part = paired[..., 1]
    turned = jnp.stack(
        [even_part * cosine - odd_part * sine, even_part * sine + odd_part * cosine], axis=-1
    )
    return turned.reshape(field.shape)


def finish_rows(widened, squares, gain, angles, head_count):
    scaled = widened * lax.rsqrt(squares / D + epsilon)[:, None] * gain[None, :]
    turned = rotate(scaled.reshape(widened.shape[0], head_count, HEAD_DIM), angles)
    return turned.reshape(widened.shape).astype(jnp.bfloat16)


def local(
    queries, keys, values, query_gain, key_gain, shapes, windows, text_keys, text_values, owner
):
    row_count, feat_width = queries.shape
    head_count = feat_width // HEAD_DIM
    tile_rows = TILE_H * TILE_W
    tiles_here = row_count // tile_rows
    first_global = lax.axis_index("seq") * tiles_here
    tile_starts, tile_ends = tile_table(shapes)
    tile_ids = first_global + jnp.arange(tiles_here, dtype=jnp.int32)
    sample_ids, one_hot, frames, bands, columns = locate(tile_ids, shapes, tile_starts, tile_ends)
    angles = rope_angles(frames, bands, columns, HEAD_DIM)
    query_wide = queries.astype(jnp.float32)
    key_wide = keys.astype(jnp.float32)
    query_squares, key_squares = lax.psum(
        (jnp.sum(query_wide * query_wide, axis=1), jnp.sum(key_wide * key_wide, axis=1)), "head"
    )
    q_hat = finish_rows(query_wide, query_squares, query_gain, angles, head_count)
    k_hat = finish_rows(key_wide, key_squares, key_gain, angles, head_count)
    key_value = jnp.stack([k_hat, values])
    extended = extended_2(key_value, (("seq", 1),), REACH * tile_rows)
    panel_of_tile = jnp.sum(one_hot * owner[None, :], axis=1)
    prompt_pair = jnp.stack([text_keys, text_values])
    every_panel = lax.all_gather(prompt_pair, "seq", axis=2, tiled=True)
    wanted = jnp.stack([panel_of_tile[0], panel_of_tile[tiles_here - 1]])
    panels = jnp.take(every_panel, wanted, axis=1)
    prompt_keys = panels[0].reshape(2 * TXT, head_count, HEAD_DIM)
    prompt_values = panels[1].reshape(2 * TXT, head_count, HEAD_DIM)
    second_slot = (sample_ids != sample_ids[0]).astype(jnp.int32)
    prompt_allowed = second_slot[:, None] == (jnp.arange(2 * TXT, dtype=jnp.int32) // TXT)[None, :]
    key_tiles = first_global - REACH + jnp.arange(tiles_here + 2 * REACH, dtype=jnp.int32)
    window_allowed = (
        jnp.any(windows[:, :, None] == key_tiles[None, None, :], axis=1) & (key_tiles >= 0)[None, :]
    )
    group_tiles = 4
    span_tiles = group_tiles + 2 * REACH
    group_rows = group_tiles * tile_rows
    factor = HEAD_DIM ** (-0.5)

    def attend(block_index):
        start_tile = block_index * group_tiles
        query_rows = lax.dynamic_slice_in_dim(q_hat, start_tile * tile_rows, group_rows, 0).reshape(
            group_rows, head_count, HEAD_DIM
        )
        key_rows = lax.dynamic_slice_in_dim(
            extended[0], start_tile * tile_rows, span_tiles * tile_rows, 0
        ).reshape(span_tiles * tile_rows, head_count, HEAD_DIM)
        value_rows = lax.dynamic_slice_in_dim(
            extended[1], start_tile * tile_rows, span_tiles * tile_rows, 0
        ).reshape(span_tiles * tile_rows, head_count, HEAD_DIM)
        allowed = lax.dynamic_slice(
            window_allowed, (start_tile, start_tile), (group_tiles, span_tiles)
        )
        prompt_ok = lax.dynamic_slice_in_dim(prompt_allowed, start_tile, group_tiles, 0)
        key_mask = jnp.concatenate(
            [
                jnp.repeat(jnp.repeat(allowed, tile_rows, axis=0), tile_rows, axis=1),
                jnp.repeat(prompt_ok, tile_rows, axis=0),
            ],
            axis=1,
        )
        all_keys = jnp.concatenate([key_rows, prompt_keys], axis=0)
        all_values = jnp.concatenate([value_rows, prompt_values], axis=0)
        scores = (
            jnp.einsum("qhd,khd->hqk", query_rows, all_keys, preferred_element_type=jnp.float32)
            * factor
        )
        scores = jnp.where(key_mask[None, :, :], scores, -jnp.inf)
        largest = jnp.max(scores, axis=-1, keepdims=True)
        weights = jnp.exp(scores - largest)
        totals = jnp.sum(weights, axis=-1)
        mixed = jnp.einsum(
            "hqk,khd->qhd",
            weights.astype(jnp.bfloat16),
            all_values,
            preferred_element_type=jnp.float32,
        )
        mixed = mixed / jnp.transpose(totals)[:, :, None]
        return mixed.astype(jnp.bfloat16).reshape(group_rows, feat_width)

    outputs = lax.map(attend, jnp.arange(tiles_here // group_tiles, dtype=jnp.int32))
    return outputs.reshape(row_count, feat_width)


def solution(mesh):
    placed = (
        P("seq", "head"),
        P("seq", "head"),
        P("seq", "head"),
        P("head"),
        P("head"),
        P(),
        P("seq", None),
        P(None, "seq", "head"),
        P(None, "seq", "head"),
        P(),
    )
    return jax.shard_map(
        local, mesh=mesh, in_specs=placed, out_specs=P("seq", "head"), check_vma=False
    )
```

profile of v0, /device:TPU:1, one launch (start us, length us, event | category | flops | bytes accessed | tf_op | source)
XLA Modules:
  0.0 366.4 jit_solution(5512880522823748688)
XLA Ops:
  6.5 2.1 pad_maximum_fusion.4
  9.4 15.2 %all-reduce = (f32[1024]{0:T(1024)S(1)}, f32[1024]{0:T(1024)S(1)}) all-reduce(f32[1024]{0:T(1024)S(1)} %fusion.26, f32[1024]{0:T(1024)S(1)} %fusion.28), channel_id=1, replica_groups=mesh['seq'=32,'head'=8] {'head'}, use_global_device_ids=true, to_apply=%region_8.9 | all-reduce | flops 2048 | bytes 16384 | tf_op jit(solution)/shard_map/psum | solution.py:106
  26.3 2.1 copy.28
  28.4 4.5 %reshape_reshape.8 = f32[1024,5,64,2]{0,3,2,1:T(2,128)} reshape(f32[1024,640]{0,1:T(8,128)} %copy.28) | data formatting | bytes 5242880 | tf_op jit(solution)/shard_map/reshape;reshape | solution.py:75
  34.6 2.1 copy.31
  36.7 4.6 %reshape_reshape.9 = f32[1024,5,64,2]{0,3,2,1:T(2,128)} reshape(f32[1024,640]{0,1:T(8,128)} %copy.31) | data formatting | bytes 5242880 | tf_op jit(solution)/shard_map/reshape;reshape | solution.py:75
  43.7 9.1 %subtract_convert_fusion = (bf16[1024,5,64,1]{0,3,2,1:T(2,128)(2,1)}, bf16[1024,5,64,1]{0,3,2,1:T(2,128)(2,1)}, bf16[1024,5,64,1]{0,3,2,1:T(2,128)(2,1)S(1)}, bf16[1024,5,64,1]{0,3,2,1:T(2,128)(2,1)S(1)}) fusion(f32[1024,5,64,2]{0,3,2,1:T(2,128)} %reshape_reshape.9, f32[1024,64]{0,1:T(8,128)S(1)} %get-tuple-element.183, ...), kind=kLoop, calls=%fused_computation.46 | loop fusion | flops 5242880 | bytes 8388608 | tf_op jit(solution)/shard_map/convert.2
  52.8 3.0 pad_maximum_fusion.2
  58.0 2.4 fusion.30
  60.4 3.5 collective-permute-start
  65.3 5.8 %pad_maximum_fusion.3 = bf16[1024,5,64,2]{0,3,2,1:T(2,128)(2,1)} fusion(bf16[1024,5,64,1]{0,3,2,1:T(2,128)(2,1)} %get-tuple-element.173, bf16[1024,5,64,1]{0,3,2,1:T(2,128)(2,1)} %get-tuple-element.172), kind=kLoop, calls=%fused_computation.43 | loop fusion | flops 2621440 | bytes 2621440 | tf_op jit(solution)/shard_map/stack | solution.py:80
  71.1 4.1 %convert_element_type.86 = bf16[1024,640]{0,1:T(8,128)(2,1)} reshape(bf16[1024,5,64,2]{0,3,2,1:T(2,128)(2,1)} %pad_maximum_fusion.3) | data formatting | bytes 2621440 | tf_op jit(solution)/shard_map/convert_element_type | solution.py:89
  79.3 69.1 %collective-permute-done = bf16[2,896,640]{1,2,0:T(8,128)(2,1)} collective-permute-done((bf16[2,896,640]{1,2,0:T(8,128)(2,1)}, bf16[2,896,640]{1,2,0:T(8,128)(2,1)}, u32[]{:S(2)}, u32[]{:S(2)}) %collective-permute-start) | collective-permute-done | bytes 2293792 | tf_op jit(solution)/shard_map/ppermute | solution.py:25
  148.4 10.5 %collective-permute-done.1 = bf16[2,896,640]{1,2,0:T(8,128)(2,1)} collective-permute-done((bf16[2,896,640]{1,2,0:T(8,128)(2,1)}, bf16[2,896,640]{1,2,0:T(8,128)(2,1)}, u32[]{:S(2)}, u32[]{:S(2)}) %collective-permute-start.1) | collective-permute-done | bytes 2293792 | tf_op jit(solution)/shard_map/ppermute | solution.py:27
  158.9 5.7 %pad_maximum_fusion = bf16[2,2816,640]{1,2,0:T(8,128)(2,1)} fusion(bf16[2,896,640]{1,2,0:T(8,128)(2,1)} %collective-permute-done.1, bf16[1,1024,640]{1,2,0:T(8,128)(2,1)S(1)} %bitcast.119, bf16[1,1024,640]{1,2,0:T(8,128)(2,1)S(1)} %convert_element_type.83, bf16[2,896,640]{1,2,0:T(8,128)(2,1)} %collective-permute-done), kind=kLoop, calls=%fused_computation.29 | loop fusion | flops 28835840 | bytes 14417920 | tf_op jit(solution)/shard_map/concatenate | solution.py:23
  164.7 57.8 %all-gather.2.cloned.1.call-done = bf16[2,32,256,640]{3,2,1,0:T(8,128)(2,1)} async-done(((bf16[2,32,8,640]{3,2,1,0:T(8,128)(2,1)}), bf16[2,32,256,640]{3,2,1,0:T(8,128)(2,1)}) %all-gather.2.cloned.1.call-update) | async-done | bytes 20971536 | tf_op jit(solution)/shard_map/all_gather | solution.py:115
  222.5 7.7 %gather_fusion = bf16[2,2,256,640]{3,2,1,0:T(8,128)(2,1)S(1)} fusion(bf16[2,32,256,640]{3,2,1,0:T(8,128)(2,1)} %all-gather.2.cloned.1.call-done, s32[1024]{0:T(1024)S(1)} %pad_clamp_fusion), kind=kCustom, calls=%fused_computation | custom fusion | bytes 2621448 | tf_op jit(solution)/shard_map/jit(_take)/gather | solution.py:117
  234.4 125.1 %while.12 = (s32[]{:T(128)}, bf16[2,512,640]{2,1,0:T(8,128)(2,1)}, bf16[2,2816,640]{1,2,0:T(8,128)(2,1)}, s32[2]{0:T(128)S(1)}, bf16[512,5,128]{0,2,1:T(8,128)(2...) while((s32[]{:T(128)}, bf16[2,512,640]{2,1,0:T(8,128)(2,1)}, ...), condition=%wide.region_14.15_spmd, body=%wide.region_11.14_spmd.sunk | while | flops 3786796032 | bytes 151642208 | solution.py:172
  238.7 3.2 copy.51
  242.7 3.6 fusion.54
  246.3 2.0 constant_dynamic-slice_fusion.9
  248.3 3.3 copy.52
  252.8 15.2 %fusion.55 = (f32[5,512]{1,0:T(8,128)S(1)}, f32[5,512,2816]{2,1,0:T(8,128)}) fusion(pred[512,2816]{1,0:T(8,128)(4,1)} %copy.51, bf16[512,5,128]{0,2,1:T(8,128)(2,1)S(1)} %bitcast.117, bf16[512,5,128]{2,0,1:T(8,128)(2,1)} %get-tuple-element.304, bf16[2304,5,128]{2,0,1:T(8,128)(2,1)} %copy.52), kind=kOutput, calls=%fused_computation.3.clone.1 | convolution fusion | flops 1874327040 | bytes 34547712 | tf_op jit(solution)/shard_map/while/body/eval_jaxpr/qhd,khd->hqk/dot_general | solution.py:156
  268.0 13.8 %fusion.56 = f32[5,512]{1,0:T(8,128)S(1)} fusion(f32[5,512,2816]{2,1,0:T(8,128)} %get-tuple-element.257, f32[5,512]{1,0:T(8,128)S(1)} %get-tuple-element.258, pred[512,2816]{1,0:T(8,128)(4,1)S(1)} %copy-done), kind=kLoop, calls=%fused_computation.4.clone.1 | loop fusion | flops 28833280 | bytes 30298112 | tf_op jit(solution)/shard_map/while/body/eval_jaxpr/reduce_sum | solution.py:162
  281.7 14.1 %divide_convert_fusion.2 = bf16[512,5,128]{0,2,1:T(8,128)(2,1)S(1)} fusion(f32[512,5]{0,1:T(8,128)S(1)} %bitcast.122, f32[5,512,2816]{2,1,0:T(8,128)} %get-tuple-element.257, f32[5,512]{1,0:T(8,128)S(1)} %get-tuple-element.258, pred[512,2816]{1,0:T(8,128)(4,1)S(1)} %copy-done, bf16[512,5,128]{0,2,1:T(8,128)(2,1)S(1)} %copy-done.4, ...), kind=kOutput, calls=%fused_computation.17.clone.1 | convolution fusion | flops 1882193920 | bytes 34557952 | tf_op jit(solution)/shard_map/while/body/eval_jaxpr/hqk,khd->qhd/dot_general | solution.py:163
  301.3 3.2 copy.51
  305.2 3.6 fusion.54
  308.8 2.0 constant_dynamic-slice_fusion.9
  310.9 3.3 copy.52
  315.3 15.2 %fusion.55 = (f32[5,512]{1,0:T(8,128)S(1)}, f32[5,512,2816]{2,1,0:T(8,128)}) fusion(pred[512,2816]{1,0:T(8,128)(4,1)} %copy.51, bf16[512,5,128]{0,2,1:T(8,128)(2,1)S(1)} %bitcast.117, bf16[512,5,128]{2,0,1:T(8,128)(2,1)} %get-tuple-element.304, bf16[2304,5,128]{2,0,1:T(8,128)(2,1)} %copy.52), kind=kOutput, calls=%fused_computation.3.clone.1 | convolution fusion | flops 1874327040 | bytes 34547712 | tf_op jit(solution)/shard_map/while/body/eval_jaxpr/qhd,khd->hqk/dot_general | solution.py:156
  330.5 13.8 %fusion.56 = f32[5,512]{1,0:T(8,128)S(1)} fusion(f32[5,512,2816]{2,1,0:T(8,128)} %get-tuple-element.257, f32[5,512]{1,0:T(8,128)S(1)} %get-tuple-element.258, pred[512,2816]{1,0:T(8,128)(4,1)S(1)} %copy-done), kind=kLoop, calls=%fused_computation.4.clone.1 | loop fusion | flops 28833280 | bytes 30298112 | tf_op jit(solution)/shard_map/while/body/eval_jaxpr/reduce_sum | solution.py:162
  344.3 14.1 %divide_convert_fusion.2 = bf16[512,5,128]{0,2,1:T(8,128)(2,1)S(1)} fusion(f32[512,5]{0,1:T(8,128)S(1)} %bitcast.122, f32[5,512,2816]{2,1,0:T(8,128)} %get-tuple-element.257, f32[5,512]{1,0:T(8,128)S(1)} %get-tuple-element.258, pred[512,2816]{1,0:T(8,128)(4,1)S(1)} %copy-done, bf16[512,5,128]{0,2,1:T(8,128)(2,1)S(1)} %copy-done.4, ...), kind=kOutput, calls=%fused_computation.17.clone.1 | convolution fusion | flops 1882193920 | bytes 34557952 | tf_op jit(solution)/shard_map/while/body/eval_jaxpr/hqk,khd->qhd/dot_general | solution.py:163
  (96 shorter events, 30.0 us)
Async XLA Ops:
  6.5 2.2 copy-start.2
  6.5 2.5 copy-start.3
  6.5 18.1 %copy-start.7 = (f32[640]{0:T(1024)S(1)}, f32[640]{0:T(1024)}, u32[]{:S(2)}) copy-start(f32[640]{0:T(1024)} %param.16) | copy-start | bytes 7684
  6.5 215.9 %all-gather.2.cloned.1.call-start = ((), (), s32[]{:S(2)}) async-start(), calls=%async_computation | async-start | bytes 21626880 | tf_op jit(solution)/shard_map/all_gather | solution.py:115
  28.4 4.5 %copy-start.8 = (f32[640]{0:T(1024)S(1)}, f32[640]{0:T(1024)}, u32[]{:S(2)}) copy-start(f32[640]{0:T(1024)} %param.15) | copy-start | bytes 7684
  36.7 4.6 %copy-start.5 = (s32[8,3]{0,1:T(4,128)S(1)}, s32[8,3]{0,1:T(4,128)}, u32[]{:S(2)}) copy-start(s32[8,3]{0,1:T(4,128)} %param.17) | copy-start | bytes 292
  36.7 5.0 %copy-start.9 = (s32[8]{0:T(128)S(1)}, s32[8]{0:T(128)}, u32[]{:S(2)}) copy-start(s32[8]{0:T(128)} %param.21) | copy-start | bytes 100
  36.7 7.0 %copy-start.1 = (f32[1024,5,64,2]{0,3,2,1:T(2,128)S(1)}, f32[1024,5,64,2]{0,3,2,1:T(2,128)}, u32[]{:S(2)}) copy-start(f32[1024,5,64,2]{0,3,2,1:T(2,128)} %reshape_reshape.8) | copy-start | bytes 7864324
  60.4 88.1 %collective-permute-start = (bf16[2,896,640]{1,2,0:T(8,128)(2,1)}, bf16[2,896,640]{1,2,0:T(8,128)(2,1)}, u32[]{:S(2)}, u32[]{:S(2)}) collective-permute-start(bf16[2,896,640]{1,2,0:T(8,128)(2,1)} %get-tuple-element.176), channel_id=1, source_target_pairs={{0,8},{8,16},{16,24},{24,32},{32,40},{40,48},{48,56},{56,64},{64,7... | collective-permute-start | bytes 6881288 | tf_op jit(solution)/shard_map/ppermute | solution.py:25
  63.8 95.1 %collective-permute-start.1 = (bf16[2,896,640]{1,2,0:T(8,128)(2,1)}, bf16[2,896,640]{1,2,0:T(8,128)(2,1)}, u32[]{:S(2)}, u32[]{:S(2)}) collective-permute-start(bf16[2,896,640]{1,2,0:T(8,128)(2,1)} %get-tuple-element.177), channel_id=1, source_target_pairs={{8,0},{16,8},{24,16},{32,24},{40,32},{48,40},{56,48},{64,56},{72,6... | collective-permute-start | bytes 6881288 | tf_op jit(solution)/shard_map/ppermute | solution.py:27
  65.3 13.2 %copy-start.6 = (s32[8,27]{1,0:T(8,128)S(1)}, s32[8,27]{1,0:T(8,128)}, u32[]{:S(2)}) copy-start(s32[8,27]{1,0:T(8,128)} %param.18) | copy-start | bytes 2596
  252.8 15.2 %copy-start = (pred[512,2816]{1,0:T(8,128)(4,1)S(1)}, pred[512,2816]{1,0:T(8,128)(4,1)}, u32[]{:S(2)}) copy-start(pred[512,2816]{1,0:T(8,128)(4,1)} %copy.51) | copy-start | bytes 4325380 | tf_op jit(solution)/shard_map/while
  268.0 13.8 %copy-start.4 = (bf16[512,5,128]{0,2,1:T(8,128)(2,1)S(1)}, bf16[512,5,128]{0,2,1:T(8,128)(2,1)}, u32[]{:S(2)}) copy-start(bf16[512,5,128]{0,2,1:T(8,128)(2,1)} %get-tuple-element.300) | copy-start | bytes 1966084 | tf_op jit(solution)/shard_map/while
  315.3 15.2 %copy-start = (pred[512,2816]{1,0:T(8,128)(4,1)S(1)}, pred[512,2816]{1,0:T(8,128)(4,1)}, u32[]{:S(2)}) copy-start(pred[512,2816]{1,0:T(8,128)(4,1)} %copy.51) | copy-start | bytes 4325380 | tf_op jit(solution)/shard_map/while
  330.5 13.8 %copy-start.4 = (bf16[512,5,128]{0,2,1:T(8,128)(2,1)S(1)}, bf16[512,5,128]{0,2,1:T(8,128)(2,1)}, u32[]{:S(2)}) copy-start(bf16[512,5,128]{0,2,1:T(8,128)(2,1)} %get-tuple-element.300) | copy-start | bytes 1966084 | tf_op jit(solution)/shard_map/while
Sparse Core Ops, SparseCore 0:
  10.0 212.3 all-gather.1
where the time goes:
time: 367 us; the launch traced here: 366 us
  waiting for transfers between devices  137 us (37%)
  local copies, waits for them, and re-layouts  67.2 us (18%)
  other arithmetic  66.6 us (18%)
  matrix products  58.5 us (16%)
  blocking collectives  15.2 us (4%)
  between operations  13.6 us (4%)
  starting transfers between devices  4.92 us (1%)
    ppermute x1, waiting for transfers between devices, extended_2(): lax.ppermute(tail, axis, [(i, (i + 1) % count) for i in range(ends)])  69.1 us
    all_gather x1, waiting for transfers between devices, local(): every_panel = lax.all_gather(prompt_pair, 'seq', axis=2, tiled=True)  57.8 us
    dot_general x2, matrix products, attend(): jnp.einsum('qhd,khd->hqk', query_rows, all_keys, preferred_element_type=j...  30.4 us
    dot_general x2, matrix products, attend(): jnp.einsum('hqk,khd->qhd', weights.astype(jnp.bfloat16), all_values, pref...  28.1 us
    reduce_sum x2, other arithmetic, attend(): totals = jnp.sum(weights, axis=-1)  27.5 us
    psum x1, blocking collectives, local(): lax.psum((jnp.sum(query_wide * query_wide, axis=1), jnp.sum(key_wide * ke...  15.2 us
    ppermute x1, waiting for transfers between devices, extended_2(): lax.ppermute(head, axis, [((i + 1) % count, i) for i in range(ends)])  10.5 us
    another operation x2, other arithmetic  9.31 us
  transfers between devices with their start and end apart: 3, of which 3 were waited for; matrix products, arithmetic and copies ran while one was open for 15% of the time, Pallas kernels for 0%

commit v1 on v0

v1 whole, which is shorter than its diff:
```python
import jax
import jax.numpy as jnp
import numpy as np
from jax import lax
from jax.experimental import pallas as pl
from jax.experimental.pallas import tpu as pltpu
from jax.sharding import PartitionSpec as P

MESH = pl.DeviceIdType.MESH
HEAD_DIM = 128
D = 5120
TILE = 128
FRAME = 512
ROWS = 1024
HEADS = 5
TXT = 256
PANELS = 32
SAMPLES = 8
SEQ = 32
HEAD = 8
TXT_ROWS = 8
EPSILON = 1e-06
MASKED = -1e30
TIMES = 16


def rope_tables():
    third = HEAD_DIM // 6
    sizes = (HEAD_DIM - 4 * third, 2 * third, 2 * third)
    lane = np.arange(HEAD_DIM)
    parts = []
    start = 0
    for size, count in zip(sizes, (TIMES, 32, 32)):
        frequency = (np.float32(10000.0) ** (-np.arange(0, size, 2, dtype=np.float32) / np.float32(size))).astype(np.float32)
        angle = np.arange(count, dtype=np.float32)[:, None] * frequency[None, :]
        cosine = np.zeros((count, HEAD_DIM), np.float32)
        sine = np.zeros((count, HEAD_DIM), np.float32)
        cosine[:, start : start + size] = np.repeat(np.cos(angle), 2, axis=1)
        sine[:, start : start + size] = np.repeat(np.sin(angle), 2, axis=1)
        even = lane % 2 == 0
        parts.append(np.stack([cosine, np.where(even, -sine, 0.0), np.where(even, 0.0, sine)]).astype(np.float32))
        start += size
    time, row, col = parts
    return time, row.reshape(3, 4, 8, HEAD_DIM), col.reshape(3, 2, 16, HEAD_DIM)


def kernel(
    shapes, windows, owner, query_gain, key_gain, time_tab, row_tab, col_tab,
    q_hbm, k_hbm, v_hbm, tk_hbm, tv_hbm, out_hbm,
    qx, kx, vx, text, send, got, hk, hv, squares, peer_squares, totals, halo_totals,
    inverse, cos_h, sina_h, sinb_h, inv_h, outs, bias,
    load_sem, halo_send, halo_recv, sq_send, sq_recv, tot_send, tot_recv, txt_send, txt_recv, own_sem, out_sem,
):
    seq = lax.axis_index("seq")
    head = lax.axis_index("head")
    right = lax.rem(seq + 1, SEQ)
    left = lax.rem(seq + SEQ - 1, SEQ)

    loads = []
    for h in range(HEADS):
        lanes = pl.ds(h * HEAD_DIM, HEAD_DIM)
        loads.append(pltpu.make_async_copy(k_hbm.at[:, lanes], kx.at[h], load_sem.at[0, h]))
        loads.append(pltpu.make_async_copy(q_hbm.at[:, lanes], qx.at[h], load_sem.at[1, h]))
        loads.append(pltpu.make_async_copy(v_hbm.at[:, lanes], vx.at[h], load_sem.at[2, h]))
    loads.append(pltpu.make_async_copy(tk_hbm, text.at[0], load_sem.at[0, HEADS]))
    loads.append(pltpu.make_async_copy(tv_hbm, text.at[1], load_sem.at[1, HEADS]))
    for load in loads:
        load.start()

    barrier = pltpu.get_barrier_semaphore()

    def greet_seq(j, carry):
        pl.semaphore_signal(barrier, inc=1, device_id={"seq": lax.rem(seq + j, SEQ), "head": head}, device_id_type=MESH)
        return carry

    def greet_head(j, carry):
        pl.semaphore_signal(barrier, inc=1, device_id={"seq": seq, "head": lax.rem(head + j, HEAD)}, device_id_type=MESH)
        return carry

    lax.fori_loop(1, SEQ, greet_seq, 0)
    lax.fori_loop(1, HEAD, greet_head, 0)
    for load in loads:
        load.wait()

    def square_tile(i, carry):
        at = pl.ds(pl.multiple_of(i * TILE, TILE), TILE)
        for base, x in ((0, qx), (8, kx)):
            total = jnp.zeros((TILE, HEAD_DIM), jnp.float32)
            for h in range(HEADS):
                wide = x[h, at, :].astype(jnp.float32)
                total = total + wide * wide
            squares[pl.ds(base + i, 1), :] = jnp.sum(total.T, axis=0, keepdims=True)
        return carry

    lax.fori_loop(0, 8, square_tile, 0)
    pl.semaphore_wait(barrier, SEQ - 1 + HEAD - 1)

    def halo_copy(h, kv, direction):
        source = (k_hbm, v_hbm)[kv]
        target = (hk, hv)[kv]
        lanes = pl.ds(pl.multiple_of(h * HEAD_DIM, HEAD_DIM), HEAD_DIM)
        return pltpu.make_async_remote_copy(
            src_ref=source.at[pl.ds((1 - direction) * FRAME, FRAME), lanes],
            dst_ref=target.at[direction, h],
            send_sem=halo_send.at[direction, kv, h],
            recv_sem=halo_recv.at[direction, kv, h],
            device_id={"seq": (right, left)[direction], "head": head},
            device_id_type=MESH,
        )

    def halo_start(h, carry):
        for kv in range(2):
            for direction in range(2):
                halo_copy(h, kv, direction).start()
        return carry

    def square_copy(j):
        return pltpu.make_async_remote_copy(
            src_ref=squares,
            dst_ref=peer_squares.at[j - 1],
            send_sem=sq_send.at[j - 1],
            recv_sem=sq_recv.at[j - 1],
            device_id={"seq": seq, "head": lax.rem(head + j, HEAD)},
            device_id_type=MESH,
        )

    def text_copy(j):
        to = lax.rem(seq + j, SEQ)
        return pltpu.make_async_remote_copy(
            src_ref=send.at[to],
            dst_ref=got.at[seq],
            send_sem=txt_send.at[j],
            recv_sem=txt_recv.at[j],
            device_id={"seq": to, "head": head},
            device_id_type=MESH,
        )

    def start_of(copy):
        def body(j, carry):
            copy(j).start()
            return carry
        return body

    def wait_of(copy):
        def body(j, carry):
            copy(j).wait()
            return carry
        return body

    lax.fori_loop(1, HEAD, start_of(square_copy), 0)
    halo_start(0, 0)

    frames = [shapes[s, 0] for s in range(SAMPLES)]
    ends = []
    running = jnp.int32(0)
    for s in range(SAMPLES):
        running = running + frames[s]
        ends.append(running)

    def video_of(frame):
        sample = jnp.int32(0)
        first = jnp.int32(0)
        for s in range(SAMPLES - 1):
            past = frame >= ends[s]
            sample = sample + jnp.where(past, 1, 0)
            first = first + jnp.where(past, frames[s], 0)
        return sample, first

    def pack(e, carry):
        for slot in range(2):
            sample, _ = video_of(2 * e + slot)
            panel = owner[sample]
            for kv in range(2):
                send[e, slot, kv] = text[kv, panel]
        return carry

    lax.fori_loop(0, SEQ, pack, 0)

    places = []
    for offset in (-1, 0, 1, 2):
        frame = lax.rem(2 * seq + offset + 2 * SEQ, 2 * SEQ)
        sample, first = video_of(frame)
        places.append((jnp.clip(frame - first, 0, TIMES - 1), shapes[sample, 2] > 16))

    for i in range(8):
        at, land = i % 4, places[1 + i // 4][1]
        for step in range(3):
            for other in range(4):
                wide_slot = step * 9 + (other // 2 - at // 2 + 1) * 3 + (other % 2 - at % 2 + 1)
                listed = windows[i, wide_slot]
                if abs(other - at) <= 1:
                    listed_tall = windows[i, step * 9 + (other - at + 1) * 3 + 1]
                else:
                    listed_tall = jnp.int32(-1)
                chosen = jnp.where(land, listed, listed_tall)
                bias[i * 12 + step * 4 + other] = jnp.where(chosen >= 0, jnp.float32(0.0), jnp.float32(MASKED))

    lax.fori_loop(1, HEAD, wait_of(square_copy), 0)
    whole = squares[...]
    for j in range(HEAD - 1):
        whole = whole + peer_squares[j]
    totals[...] = whole[8:16]

    def total_copy(direction):
        return pltpu.make_async_remote_copy(
            src_ref=totals,
            dst_ref=halo_totals.at[direction],
            send_sem=tot_send.at[direction],
            recv_sem=tot_recv.at[direction],
            device_id={"seq": (right, left)[direction], "head": head},
            device_id_type=MESH,
        )

    inverse[...] = lax.rsqrt(whole / D + EPSILON)
    for direction in range(2):
        total_copy(direction).start()
    own_text = pltpu.make_async_copy(send.at[seq], got.at[seq], own_sem)
    own_text.start()
    lax.fori_loop(1, SEQ, start_of(text_copy), 0)
    lax.fori_loop(1, HEADS, halo_start, 0)

    def tables(place, w):
        t, land = place
        b = jnp.where(land, w // 2, w)
        c = jnp.where(land, lax.rem(w, 2), 0)
        made = []
        for n in range(3):
            rest = col_tab[n, c] + time_tab[n, pl.ds(t, 1), :]
            rows = row_tab[n, b]
            made.append(jnp.concatenate([rows[a : a + 1] + rest for a in range(8)], axis=0))
        return made

    def column(row):
        return jnp.broadcast_to(row, (TILE, HEAD_DIM)).T

    def turned(x, inv, gain, cosine, sine_a, sine_b):
        y = x.astype(jnp.float32) * inv * gain
        return (y * cosine + pltpu.roll(y, HEAD_DIM - 1, 1) * sine_a + pltpu.roll(y, 1, 1) * sine_b).astype(jnp.bfloat16)

    for frame in range(2):
        def prepare(w, carry, frame=frame):
            i = frame * 4 + w
            at = pl.ds(pl.multiple_of(i * TILE, TILE), TILE)
            tabs = tables(places[1 + frame], w)
            inv_q = column(inverse[pl.ds(i, 1), :])
            inv_k = column(inverse[pl.ds(8 + i, 1), :])
            for h in range(HEADS):
                qx[h, at, :] = turned(qx[h, at, :], inv_q, query_gain[h : h + 1, :], *tabs)
                kx[h, at, :] = turned(kx[h, at, :], inv_k, key_gain[h : h + 1, :], *tabs)
            return carry
        lax.fori_loop(0, 4, prepare, 0)

    for direction in range(2):
        total_copy(direction).wait()
    halo_inverse = lax.rsqrt(halo_totals[...] / D + EPSILON)
    halo_totals[...] = halo_inverse
    for direction in range(2):
        def prepare_halo(w, carry, direction=direction):
            cosine, sine_a, sine_b = tables(places[3 * direction], w)
            i = direction * 4 + w
            cos_h[i] = cosine
            sina_h[i] = sine_a
            sinb_h[i] = sine_b
            inv_h[i] = column(halo_totals[direction, pl.ds((1 - direction) * 4 + w, 1), :])
            return carry
        lax.fori_loop(0, 4, prepare_halo, 0)

    lax.fori_loop(1, SEQ, wait_of(text_copy), 0)
    own_text.wait()

    sharp = np.float32(HEAD_DIM ** -0.5 * np.log2(np.e))
    last_dims = (((1,), (1,)), ((), ()))

    def out_copy(h, frame):
        return pltpu.make_async_copy(
            outs.at[h, pl.ds(frame * FRAME, FRAME), :],
            out_hbm.at[pl.ds(frame * FRAME, FRAME), pl.ds(pl.multiple_of(h * HEAD_DIM, HEAD_DIM), HEAD_DIM)],
            out_sem.at[h, frame],
        )

    def attend(h, carry):
        for kv in range(2):
            for direction in range(2):
                halo_copy(h, kv, direction).wait()
        gain = key_gain[pl.ds(h, 1), :]
        for direction in range(2):
            for w in range(4):
                i = direction * 4 + w
                at = pl.ds(w * TILE, TILE)
                hk[direction, h, at, :] = turned(hk[direction, h, at, :], inv_h[i], gain, cos_h[i], sina_h[i], sinb_h[i])
        lanes = pl.ds(pl.multiple_of(h * HEAD_DIM, HEAD_DIM), HEAD_DIM)
        for frame in range(2):
            text_k = got[:, frame, 0, :, lanes].reshape(TXT, HEAD_DIM)
            text_v = got[:, frame, 1, :, lanes].reshape(TXT, HEAD_DIM)
            if frame == 0:
                keys = (hk[0, h], kx[h], text_k)
                values = (hv[0, h], vx[h], text_v)
            else:
                keys = (kx[h], hk[1, h], text_k)
                values = (vx[h], hv[1, h], text_v)
            for half in range(2):
                first = frame * FRAME + half * 256
                q = qx[h, pl.ds(first, 256), :]
                scores = jnp.concatenate(
                    [lax.dot_general(q, k, last_dims, preferred_element_type=jnp.float32) for k in keys], axis=1
                )
                masked = []
                for part in range(2):
                    i = frame * 4 + half * 2 + part
                    band = scores[part * TILE : (part + 1) * TILE]
                    pieces = [band[:, j * TILE : (j + 1) * TILE] + bias[i * 12 + j] for j in range(12)]
                    masked.append(jnp.concatenate(pieces + [band[:, 12 * TILE :]], axis=1))
                scores = jnp.concatenate(masked, axis=0)
                largest = jnp.max(scores, axis=1, keepdims=True)
                weights = jnp.exp2((scores - largest) * sharp)
                total = jnp.sum(weights, axis=1, keepdims=True)
                weights = weights.astype(jnp.bfloat16)
                mixed = jnp.zeros((256, HEAD_DIM), jnp.float32)
                begin = 0
                for v in values:
                    mixed = mixed + jnp.dot(weights[:, begin : begin + v.shape[0]], v, preferred_element_type=jnp.float32)
                    begin += v.shape[0]
                outs[h, pl.ds(first, 256), :] = (mixed / total).astype(jnp.bfloat16)
            out_copy(h, frame).start()
        return carry

    lax.fori_loop(0, HEADS, attend, 0)

    def finish(h, carry):
        for frame in range(2):
            out_copy(h, frame).wait()
        return carry

    lax.fori_loop(0, HEADS, finish, 0)


def local(queries, keys, values, query_gain, key_gain, shapes, windows, text_keys, text_values, owner):
    time_tab, row_tab, col_tab = (jnp.asarray(t) for t in rope_tables())
    smem = pl.BlockSpec(memory_space=pltpu.SMEM)
    vmem = pl.BlockSpec(memory_space=pltpu.VMEM)
    hbm = pl.BlockSpec(memory_space=pl.ANY)
    bf16, f32 = jnp.bfloat16, jnp.float32
    dma = pltpu.SemaphoreType.DMA
    return pl.pallas_call(
        kernel,
        out_shape=jax.ShapeDtypeStruct((ROWS, HEADS * HEAD_DIM), bf16),
        in_specs=[smem] * 3 + [vmem] * 5 + [hbm] * 5,
        out_specs=hbm,
        scratch_shapes=[
            pltpu.VMEM((HEADS, ROWS, HEAD_DIM), bf16),
            pltpu.VMEM((HEADS, ROWS, HEAD_DIM), bf16),
            pltpu.VMEM((HEADS, ROWS, HEAD_DIM), bf16),
            pltpu.VMEM((2, PANELS, TXT_ROWS, HEADS * HEAD_DIM), bf16),
            pltpu.VMEM((SEQ, 2, 2, TXT_ROWS, HEADS * HEAD_DIM), bf16),
            pltpu.VMEM((SEQ, 2, 2, TXT_ROWS, HEADS * HEAD_DIM), bf16),
            pltpu.VMEM((2, HEADS, FRAME, HEAD_DIM), bf16),
            pltpu.VMEM((2, HEADS, FRAME, HEAD_DIM), bf16),
            pltpu.VMEM((16, HEAD_DIM), f32),
            pltpu.VMEM((HEAD - 1, 16, HEAD_DIM), f32),
            pltpu.VMEM((8, HEAD_DIM), f32),
            pltpu.VMEM((2, 8, HEAD_DIM), f32),
            pltpu.VMEM((16, HEAD_DIM), f32),
            pltpu.VMEM((8, TILE, HEAD_DIM), f32),
            pltpu.VMEM((8, TILE, HEAD_DIM), f32),
            pltpu.VMEM((8, TILE, HEAD_DIM), f32),
            pltpu.VMEM((8, TILE, HEAD_DIM), f32),
            pltpu.VMEM((HEADS, ROWS, HEAD_DIM), bf16),
            pltpu.SMEM((96,), f32),
            dma((3, HEADS + 1)),
            dma((2, 2, HEADS)),
            dma((2, 2, HEADS)),
            dma((HEAD - 1,)),
            dma((HEAD - 1,)),
            dma((2,)),
            dma((2,)),
            dma((SEQ,)),
            dma((SEQ,)),
            dma,
            dma((HEADS, 2)),
        ],
        compiler_params=pltpu.CompilerParams(
            collective_id=0, has_side_effects=True, vmem_limit_bytes=56 * 1024 * 1024
        ),
        cost_estimate=pl.CostEstimate(flops=5 * 10**9, bytes_accessed=12 * 10**6, transcendentals=10**7),
        name="window_prompt_attention",
    )(
        shapes, windows, owner,
        query_gain.reshape(HEADS, HEAD_DIM), key_gain.reshape(HEADS, HEAD_DIM),
        time_tab, row_tab, col_tab,
        queries, keys, values, text_keys, text_values,
    )


def solution(mesh):
    placed = (
        P("seq", "head"),
        P("seq", "head"),
        P("seq", "head"),
        P("head"),
        P("head"),
        P(),
        P("seq", None),
        P(None, "seq", "head"),
        P(None, "seq", "head"),
        P(),
    )
    return jax.shard_map(
        local, mesh=mesh, in_specs=placed, out_specs=P("seq", "head"), check_vma=False
    )
```

time: 367 us -> 80.2 us (0.22)
  waiting for transfers between devices: 137 us -> 0 us
  Pallas kernels: 0 us -> 76.2 us
  other arithmetic: 66.6 us -> 0 us
  local copies, waits for them, and re-layouts: 67.2 us -> 3.83 us
  matrix products: 58.5 us -> 0 us
  blocking collectives: 15.2 us -> 0 us
  between operations: 13.6 us -> 0.01 us
  starting transfers between devices: 4.92 us -> 0 us
    ppermute x2 -> x0, waiting for transfers between devices: 79.6 us -> none  [the longest x1 69.1 us: extended_2(): lax.ppermute(tail, axis, [(i, (i + 1) % count) for i in range(ends)])]
    pallas_call x0 -> x1, Pallas kernels: none -> 76.2 us  [local(): pl.pallas_call(kernel, out_shape=jax.ShapeDtypeStruct((ROWS, HEADS * HEAD...]
    dot_general x4 -> x0, matrix products: 58.5 us -> none  [the longest x2 30.4 us: attend(): jnp.einsum('qhd,khd->hqk', query_rows, all_keys, preferred_element_type=j...]
    all_gather x1 -> x0, waiting for transfers between devices: 57.8 us -> none  [local(): every_panel = lax.all_gather(prompt_pair, 'seq', axis=2, tiled=True)]
    reduce_sum x6 -> x0, other arithmetic: 28.6 us -> none  [the longest x2 27.5 us: attend(): totals = jnp.sum(weights, axis=-1)]
    another operation x6 -> x0, other arithmetic: 22.6 us -> none
    psum x1 -> x0, blocking collectives: 15.2 us -> none  [local(): lax.psum((jnp.sum(query_wide * query_wide, axis=1), jnp.sum(key_wide * ke...]
    another operation x4 -> x0, local copies, waits for them, and re-layouts: 11.1 us -> none  [the longest x2 9.09 us: rotate(): field.reshape(field.shape[0], field.shape[1], field.shape[2] // 2, 2)]
  transfers between devices with their start and end apart: 3 -> 0, of which waited for: 3 -> 0; matrix products, arithmetic and copies ran while one was open for 15% -> 0% of each run, Pallas kernels for 0% -> 0%
where the time goes in v1:
time: 80.2 us; the launch traced here: 80 us
  Pallas kernels  76.2 us (95%)
  local copies, waits for them, and re-layouts  3.83 us (5%)
    pallas_call x1, Pallas kernels, local(): pl.pallas_call(kernel, out_shape=jax.ShapeDtypeStruct((ROWS, HEADS * HEAD...  76.2 us
    unnamed x2, local copies, waits for them, and re-layouts  3.83 us

profile of v1, /device:TPU:1, one launch (start us, length us, event | category | flops | bytes accessed | tf_op | source)
XLA Modules:
  0.0 80.0 jit_solution(9855791435222435014)
XLA Ops:
  0.0 1.3 %copy.14.shapes = s32[8,3]{1,0:T(8,128)} copy(s32[8,3]{0,1:T(4,128)} %param.18) | data formatting | bytes 192 | tf_op args[5]
  1.3 76.2 %window_prompt_attention.1 = bf16[1024,640]{1,0:T(8,128)(2,1)} custom-call(s32[8,3]{1,0:T(8,128)} %copy.14.shapes, s32[8,27]{1,0:T(8,128)} %windows.1, s32[8]{0:T(128)} %owner.1, f32[5,128]{1,0:T(8,128)} %bitcast.2, f32[5,128]{1,0:T(8,128)} %bitcast.3, f32[3,16,128]{2,1,0:T(8,128)} %constant.6.clone.time_tab, f32[3,4,8,128]{3,2,1,0:T(8,128)} %constant.7.clone.row_tab, ...), custom_call_target="tpu_custom_call" | custom-call | flops 5000000000 | bytes 12000000 | tf_op jit(solution)/shard_map/window_prompt_attention/pallas_call | solution.py:344
  77.5 2.5 %copy.16 = bf16[1024,640]{1,0:T(8,128)(2,1)} copy(bf16[1024,640]{1,0:T(8,128)(2,1)} %window_prompt_attention.1) | data formatting | bytes 2621440
